TPU v7x, 256 devices: a whole 4x4x8 slice. The times are simulated.
256 devices in a mesh: grp: 8 (over y, z_lo), dev: 32 (over x, z_hi, core).
Axes of the slice: x: 4, y: 4, z: 8 (z_hi: 4, z_lo: 2; z = z_hi * 2 + z_lo), core: 2. Of those that a mesh axis runs over, the one named last changes fastest.
Arguments:
- resid: bfloat16 [32768, 1536], P(('grp', 'dev')), may hold values from -1.5 to 1.5
- queries: bfloat16 [32768, 1536], P(('grp', 'dev')), may hold values from -6 to 6
- suffix_kv: bfloat16 [32768, 2, 512], P(('grp', 'dev')), may hold values from -6 to 6
- prefix_kv: bfloat16 [8, 2048, 2, 512], P('grp', 'dev'), may hold values from -6 to 6
- segments: int32 [256, 128], P(('grp', 'dev')), may hold values from 0 to 3, never falling along the last dimension, each value on 1 to 64 neighbouring positions
- o_weight: bfloat16 [1536, 1536], P(('grp', 'dev')), may hold values from -0.15625 to 0.15625
- norm_gain: float32 [1536], replicated, may hold values from 0.25 to 1.75
- router: bfloat16 [1536, 32], replicated, may hold values from -0.15625 to 0.15625
- routes: int32 [32768, 8], P(('grp', 'dev')), may hold values from 0 to 31, all different within a row; in each aligned block of 128 rows (0 to 127, 128 to 255, ...) at most 48 rows name the same one
- w_gate_up: bfloat16 [32, 1536, 1024], P('dev', 'grp'), may hold values from -0.15625 to 0.15625
- w_down: bfloat16 [32, 512, 1536], P('dev', 'grp'), may hold values from -0.25 to 0.25
Outputs:
- layer_out: bfloat16 [32768, 1536], P(('grp', 'dev'))
Inputs may be any that keep to these rules, and one draw needn't show every extreme that they name: At most 48 of one device's routes name one expert.
All inputs are finite; a program needn't handle non-finite values.
Results may differ from a plain program's by a relative error of at most 0.012.
Values may be sent and summed in bfloat16 or wider, within the bound.
A program may use at most 128 MiB of HBM per device.

v0:
```python
import jax
import jax.numpy as jnp
from jax import lax
from jax.sharding import PartitionSpec as P

D = 1536
HEADS = 24
KVH = 8
HDIM = 64
FFE = 512
TOPK = 8
EXPERTS = 32
ATT = 1536
CAP = 48


def per_device(
    resid,
    queries,
    suffix_kv,
    prefix_kv,
    segments,
    o_weight,
    norm_gain,
    router,
    routes,
    w_gate_up,
    w_down,
):
    tok_rows = resid.shape[0]
    ratio = HEADS // KVH
    scale = 1.0 / HDIM**0.5
    query_heads = queries.reshape(tok_rows, KVH, ratio, HDIM)

    def update(carry, keys, values, mask):
        running, totals, accum = carry
        count = keys.shape[0]
        scores = (
            jnp.einsum(
                "tgrd,ngd->grtn",
                query_heads,
                keys.reshape(count, KVH, HDIM),
                preferred_element_type=jnp.float32,
            )
            * scale
        )
        if mask is not None:
            scores = jnp.where(mask[None, None], scores, jnp.float32(-1e30))
        newmax = jnp.maximum(running, jnp.max(scores, axis=-1))
        factor = jnp.exp(running - newmax)
        weights = jnp.exp(scores - newmax[..., None])
        totals = totals * factor + jnp.sum(weights, axis=-1)
        accum = accum * factor[..., None] + jnp.einsum(
            "grtn,ngd->grtd",
            weights.astype(jnp.bfloat16),
            values.reshape(count, KVH, HDIM),
            preferred_element_type=jnp.float32,
        )
        return (newmax, totals, accum)

    initial = (
        jnp.full((KVH, ratio, tok_rows), -1e30, jnp.float32),
        jnp.zeros((KVH, ratio, tok_rows), jnp.float32),
        jnp.zeros((KVH, ratio, tok_rows, HDIM), jnp.float32),
    )
    piece = lax.all_gather(prefix_kv[0], "dev", axis=0, tiled=True)
    carry = update(initial, piece[:, 0], piece[:, 1], None)
    seg_row = segments[0]
    positions = jnp.arange(tok_rows, dtype=jnp.int32)
    local_mask = (seg_row[:, None] == seg_row[None, :]) & (positions[None, :] <= positions[:, None])
    running, totals, accum = update(carry, suffix_kv[:, 0], suffix_kv[:, 1], local_mask)
    attended = (
        (accum / totals[..., None])
        .transpose(2, 0, 1, 3)
        .reshape(tok_rows, ATT)
        .astype(jnp.bfloat16)
    )
    projected = jnp.dot(
        attended,
        lax.all_gather(o_weight, ("grp", "dev"), axis=0, tiled=True),
        preferred_element_type=jnp.float32,
    )
    hidden = resid.astype(jnp.float32) + projected
    inverse = lax.rsqrt(jnp.mean(hidden * hidden, axis=-1, keepdims=True) + 1e-06)
    normed = (hidden * inverse * norm_gain).astype(jnp.bfloat16)
    logits = jnp.dot(normed, router, preferred_element_type=jnp.float32)
    expert_ids = jnp.arange(EXPERTS, dtype=jnp.int32)
    onehot = routes[:, :, None] == expert_ids[None, None, :]
    chosen = jnp.sum(jnp.where(onehot, logits[:, None, :], 0.0), axis=-1)
    sig = jax.nn.sigmoid(chosen)
    gates = (sig / jnp.sum(sig, axis=-1, keepdims=True)).astype(jnp.bfloat16)
    flat = onehot.reshape(tok_rows * TOPK, EXPERTS).astype(jnp.int32)
    before = jnp.cumsum(flat, axis=0) - flat
    slot = jnp.sum(before * flat, axis=-1).reshape(tok_rows, TOPK)
    place = routes * CAP + slot
    slot_ids = jnp.arange(EXPERTS * CAP, dtype=jnp.int32)
    hits = place[None, :, :] == slot_ids[:, None, None]
    table = jnp.sum(hits.astype(jnp.float32), axis=-1).astype(jnp.bfloat16)
    dispatch = jnp.dot(table, normed, preferred_element_type=jnp.float32).astype(jnp.bfloat16)
    dispatch = dispatch.reshape(EXPERTS, CAP, D)
    slot_count = dispatch.shape[1]
    received = lax.all_to_all(dispatch, "dev", split_axis=0, concat_axis=1, tiled=True)
    sliced = received
    gate_up = jnp.einsum(
        "erd,edf->erf",
        sliced,
        lax.all_gather(w_gate_up, "grp", axis=1, tiled=True),
        preferred_element_type=jnp.float32,
    )
    act = (jax.nn.silu(gate_up[..., :FFE]) * gate_up[..., FFE:]).astype(jnp.bfloat16)
    sliced = act
    expert_out = jnp.einsum(
        "erf,efd->erd",
        sliced,
        lax.all_gather(w_down, "grp", axis=1, tiled=True),
        preferred_element_type=jnp.float32,
    ).astype(jnp.bfloat16)
    returned = lax.all_to_all(expert_out, "dev", split_axis=1, concat_axis=0, tiled=True)
    returned = returned.reshape(EXPERTS * slot_count, D)
    back_hits = place[:, :, None] == slot_ids[None, None, :]
    ctable = jnp.sum(
        jnp.where(back_hits, gates[:, :, None].astype(jnp.float32), 0.0), axis=1
    ).astype(jnp.bfloat16)
    mixed = jnp.dot(ctable, returned, preferred_element_type=jnp.float32)
    return (hidden + mixed).astype(jnp.bfloat16)


def solution(mesh):
    return jax.shard_map(
        per_device,
        mesh=mesh,
        in_specs=(
            P(("grp", "dev"), None),
            P(("grp", "dev"), None),
            P(("grp", "dev"), None, None),
            P("grp", "dev", None, None),
            P(("grp", "dev"), None),
            P(("grp", "dev"), None),
            P(),
            P(),
            P(("grp", "dev"), None),
            P("dev", "grp", None),
            P("dev", "grp", None),
        ),
        out_specs=P(("grp", "dev"), None),
        check_vma=False,
    )
```

profile of v0, /device:TPU:1, one launch (start us, length us, event | category | flops | bytes accessed | tf_op | source)
XLA Modules:
  0.0 973.9 jit_solution(531432880128900151)
XLA Ops:
  7.4 0.7 all-gather.11.cloned.1.call-update
  8.8 0.8 copy.98
  9.8 1.2 copy.92
  11.0 1.5 fusion.54
  12.9 9.0 reduce-window.6
  22.6 0.7 multiply_add_fusion
  23.3 8.0 convert_reduce_fusion
  31.4 1.6 fusion.55
  33.0 42.5 %all-gather.11.cloned.1.call-done = bf16[1,2048,2,512]{3,2,0,1:T(2,128)(2,1)} async-done(((bf16[1,64,2,512]{3,2,0,1:T(2,128)(2,1)}), bf16[1,2048,2,512]{3,2,0,1:T(2,128)(2,1)}) %all-gather.11.cloned.1.call-update) | async-done | bytes 4194320 | tf_op jit(solution)/shard_map/all_gather | solution.py:66
  75.5 9.9 %fusion.53 = (bf16[2048,1,512]{2,1,0:T(2,128)(2,1)}, bf16[2048,1,512]{2,1,0:T(2,128)(2,1)}) fusion(bf16[2048,2,512]{2,1,0:T(2,128)(2,1)} %bitcast.137), kind=kLoop, calls=%fused_computation.72 | loop fusion | bytes 8388608 | tf_op jit(solution)/shard_map/slice | solution.py:67
  85.4 10.6 %copy.93 = bf16[2048,1,512]{0,2,1:T(8,128)(2,1)} copy(bf16[2048,1,512]{2,1,0:T(2,128)(2,1)} %get-tuple-element.8) | data formatting | bytes 4194304 | tf_op jit(solution)/shard_map/slice | solution.py:67
  96.0 9.0 copy.91
  105.0 10.1 %bitcast_reduce_fusion = (f32[8,3,128]{2,1,0:T(4,128)S(1)}, f32[8,2048,128,3]{2,1,3,0:T(8,128)}) fusion(bf16[2048,8,64,1]{0,2,3,1:T(8,128)(2,1)S(1)} %bitcast.138, bf16[128,8,3,64]{0,3,2,1:T(8,128)(2,1)S(1)} %bitcast.142), kind=kOutput, calls=%fused_computation.1 | convolution fusion | flops 817886208 | bytes 27668480 | tf_op jit(solution)/shard_map/tgrd,ngd->grtn/dot_general | solution.py:39
  115.4 10.6 %fusion.1 = f32[8,3,128]{2,1,0:T(4,128)S(1)} fusion(f32[8,2048,128,3]{2,1,3,0:T(8,128)} %get-tuple-element.17, f32[8,3,128]{2,1,0:T(4,128)S(1)} %get-tuple-element.13), kind=kLoop, calls=%fused_computation.3 | loop fusion | flops 18871296 | bytes 25190400 | tf_op jit(solution)/shard_map/reduce_sum | solution.py:52
  126.1 10.5 %fusion.30 = f32[128,8,3,64]{0,3,2,1:T(8,128)S(1)} fusion(bf16[2048,8,64,1]{0,2,3,1:T(8,128)(2,1)S(1)} %bitcast.140, f32[8,2048,128,3]{2,1,3,0:T(8,128)} %get-tuple-element.17, f32[8,3,128]{2,1,0:T(4,128)S(1)} %get-tuple-element.13, f32[128,8,3]{0,2,1:T(4,128)S(1)} %get-tuple-element.6, f32[128,8,3]{0,2,1:T(4,128)S(1)} %get-tuple-element.11), kind=kOutput, calls=%fused_computation.34 | convolution fusion | flops 824573952 | bytes 28086272 | tf_op jit(solution)/shard_map/grtn,ngd->grtd/dot_general | solution.py:53
  137.0 354.9 %all-gather.13.cloned.1.call-done = bf16[256,6,1536]{2,1,0:T(8,128)(2,1)} async-done(((bf16[1,6,1536]{2,1,0:T(8,128)(2,1)}), bf16[256,6,1536]{2,1,0:T(8,128)(2,1)}) %all-gather.13.cloned.1.call-update) | async-done | bytes 4718608 | tf_op jit(solution)/shard_map/all_gather | solution.py:80
  491.9 8.4 reshape.176
  500.4 3.2 multiply_reduce_fusion
  503.6 3.6 convolution_convert_fusion.1
  507.2 9.9 %all-to-all-start = ((bf16[32,48,1536]{2,1,0:T(8,128)(2,1)}), bf16[32,48,1536]{2,1,0:T(8,128)(2,1)}, u32[]{:S(2)}, u32[]{:S(2)}) async-start(bf16[32,48,1536]{2,1,0:T(8,128)(2,1)} %bitcast.135), calls=%async_computation | async-start | bytes 9437184 | tf_op jit(solution)/shard_map/all_to_all | solution.py:102
  518.3 160.1 %all-gather.7.cloned.1.call-done = bf16[1,1536,1024]{2,1,0:T(8,128)(2,1)} async-done(((bf16[1,192,1024]{2,1,0:T(8,128)(2,1)}), bf16[1,1536,1024]{2,1,0:T(8,128)(2,1)}) %all-gather.7.cloned.1.call-update) | async-done | bytes 3145744 | tf_op jit(solution)/shard_map/all_gather | solution.py:107
  678.4 9.8 %convolution_bitcast_fusion = f32[1,1536,1024]{2,1,0:T(8,128)} fusion(bf16[1536,1536]{1,0:T(8,128)(2,1)} %bitcast.29, bf16[1,1536,1024]{2,1,0:T(8,128)(2,1)} %all-gather.7.cloned.1.call-done), kind=kOutput, calls=%fused_computation.16 | convolution fusion | flops 4831838208 | bytes 14155776 | tf_op jit(solution)/shard_map/erd,edf->erf/dot_general | solution.py:104
  688.2 35.5 %all-gather.9.cloned.1.call-done = bf16[1,512,1536]{2,1,0:T(8,128)(2,1)} async-done(((bf16[1,64,1536]{2,1,0:T(8,128)(2,1)}), bf16[1,512,1536]{2,1,0:T(8,128)(2,1)}) %all-gather.9.cloned.1.call-update) | async-done | bytes 1572880 | tf_op jit(solution)/shard_map/all_gather | solution.py:115
  723.7 6.0 fusion.5
  729.7 52.2 %copy.124 = bf16[1,1536,1536]{2,0,1:T(2,128)(2,1)} copy(bf16[1,1536,1536]{2,1,0:T(8,128)(2,1)S(1)} %fusion.5) | data formatting | bytes 9437184 | tf_op jit(solution)/shard_map/convert_element_type | solution.py:117
  782.4 32.0 %reduce = bf16[1536,1536]{1,0:T(8,128)(2,1)} reduce(bf16[1536,1,1536]{2,1,0:T(2,128)(2,1)} %bitcast.136, bf16[]{:T(256)} %broadcast.126), dimensions={1}, to_apply=%bitcast.134.reduce_sub_computation | reduce | bytes 9437186
  814.3 8.2 reshape.181
  822.5 11.0 %all-to-all-start.1 = ((bf16[32,2,36864]{2,1,0:T(2,128)(2,1)}), bf16[32,2,36864]{2,1,0:T(2,128)(2,1)}, u32[]{:S(2)}, u32[]{:S(2)}) async-start(bf16[32,2,36864]{2,1,0:T(2,128)(2,1)} %reshape.181), calls=%async_computation.1 | async-start | bytes 9437184 | tf_op jit(solution)/shard_map/all_to_all | solution.py:118
  834.1 2.1 select_reduce_fusion
  836.2 104.9 %all-to-all-done.1 = bf16[32,2,36864]{2,1,0:T(2,128)(2,1)} async-done(((bf16[32,2,36864]{2,1,0:T(2,128)(2,1)}), bf16[32,2,36864]{2,1,0:T(2,128)(2,1)}, u32[]{:S(2)}, u32[]{:S(2)}) %all-to-all-start.1) | async-done | bytes 4718624 | tf_op jit(solution)/shard_map/all_to_all | solution.py:118
  941.0 20.2 %reshape.182 = bf16[1536,1,1536]{2,1,0:T(2,128)(2,1)} reshape(bf16[32,2,36864]{2,1,0:T(2,128)(2,1)} %all-to-all-done.1) | data formatting | bytes 9437184
  961.2 5.2 fusion.14
  (49 shorter events, 5.0 us)
Async XLA Ops:
  7.4 826.2 %copy-start = (bf16[1536,32]{0,1:T(8,128)(2,1)S(1)}, bf16[1536,32]{0,1:T(8,128)(2,1)}, u32[]{:S(2)}) copy-start(bf16[1536,32]{0,1:T(8,128)(2,1)} %param.18) | copy-start | bytes 294916
  7.4 24.0 %copy-start.6 = (s32[1,128]{1,0:T(1,128)S(1)}, s32[1,128]{1,0:T(1,128)}, u32[]{:S(2)}) copy-start(s32[1,128]{1,0:T(1,128)} %param.15) | copy-start | bytes 1540
  7.4 68.1 %all-gather.11.cloned.1.call-start = ((), (), s32[]{:S(2)}) async-start(), calls=%async_computation.4 | async-start | bytes 4325376 | tf_op jit(solution)/shard_map/all_gather | solution.py:66
  8.1 483.8 %all-gather.13.cloned.1.call-start = ((), (), s32[]{:S(2)}) async-start(), calls=%async_computation.5 | async-start | bytes 6316032 | tf_op jit(solution)/shard_map/all_gather | solution.py:80
  105.0 10.2 %copy-start.2 = (f32[8,3,128,128]{2,3,1,0:T(8,128)S(1)}, f32[8,3,128,128]{2,3,1,0:T(8,128)}, u32[]{:S(2)}) copy-start(f32[8,3,128,128]{2,3,1,0:T(8,128)} %get-tuple-element.15) | copy-start | bytes 4718596
  115.4 10.7 %copy-start.1 = (bf16[2048,1,512]{0,2,1:T(8,128)(2,1)S(1)}, bf16[2048,1,512]{0,2,1:T(8,128)(2,1)}, u32[]{:S(2)}) copy-start(bf16[2048,1,512]{0,2,1:T(8,128)(2,1)} %copy.93) | copy-start | bytes 6291460
  137.0 363.3 %copy-start.3 = (bf16[128,1536]{1,0:T(8,128)(2,1)S(1)}, bf16[128,1536]{1,0:T(8,128)(2,1)}, u32[]{:S(2)}) copy-start(bf16[128,1536]{1,0:T(8,128)(2,1)} %param.11) | copy-start | bytes 1179652
  500.3 3.3 copy-start.5
  507.2 171.2 %all-to-all-start = ((bf16[32,48,1536]{2,1,0:T(8,128)(2,1)}), bf16[32,48,1536]{2,1,0:T(8,128)(2,1)}, u32[]{:S(2)}, u32[]{:S(2)}) async-start(bf16[32,48,1536]{2,1,0:T(8,128)(2,1)} %bitcast.135), calls=%async_computation | async-start | bytes 9437184 | tf_op jit(solution)/shard_map/all_to_all | solution.py:102
  517.1 161.3 %all-gather.7.cloned.1.call-start = ((), (), s32[]{:S(2)}) async-start(), calls=%async_computation.2 | async-start | bytes 3538944 | tf_op jit(solution)/shard_map/all_gather | solution.py:107
  517.7 206.0 %all-gather.9.cloned.1.call-start = ((), (), s32[]{:S(2)}) async-start(), calls=%async_computation.3 | async-start | bytes 1769472 | tf_op jit(solution)/shard_map/all_gather | solution.py:115
  822.5 11.4 %copy-start.4 = (s32[128,8]{0,1:T(8,128)S(1)}, s32[128,8]{0,1:T(8,128)}, u32[]{:S(2)}) copy-start(s32[128,8]{0,1:T(8,128)} %param.19) | copy-start | bytes 12292
  822.5 118.6 %all-to-all-start.1 = ((bf16[32,2,36864]{2,1,0:T(2,128)(2,1)}), bf16[32,2,36864]{2,1,0:T(2,128)(2,1)}, u32[]{:S(2)}, u32[]{:S(2)}) async-start(bf16[32,2,36864]{2,1,0:T(2,128)(2,1)} %reshape.181), calls=%async_computation.1 | async-start | bytes 9437184 | tf_op jit(solution)/shard_map/all_to_all | solution.py:118
Sparse Core Ops, SparseCore 0:
  10.7 64.6 all-gather.10
  77.4 414.5 all-gather.12
Sparse Core Ops, SparseCore 1:
  519.4 159.0 all-gather.6
  680.1 43.6 all-gather.8
where the time goes:
time: 976 us; the launch traced here: 974 us
  waiting for transfers between devices  700 us (72%)
  local copies, waits for them, and re-layouts  124 us (13%)
  other arithmetic  63.1 us (6%)
  matrix products  50.7 us (5%)
  starting transfers between devices  21 us (2%)
  between operations  15.1 us (2%)
    all_gather x1, waiting for transfers between devices, per_device(): lax.all_gather(o_weight, ('grp', 'dev'), axis=0, tiled=True)  355 us
    all_gather x1, waiting for transfers between devices, per_device(): lax.all_gather(w_gate_up, 'grp', axis=1, tiled=True)  160 us
    all_to_all x1, waiting for transfers between devices, per_device(): lax.all_to_all(expert_out, 'dev', split_axis=1, concat_axis=0, tiled=True)  105 us
    convert_element_type x1, local copies, waits for them, and re-layouts, per_device(): expert_out = jnp.einsum('erf,efd->erd', sliced, lax.all_gather(w_down, 'g...  52.2 us
    all_gather x1, waiting for transfers between devices, per_device(): piece = lax.all_gather(prefix_kv[0], 'dev', axis=0, tiled=True)  42.5 us
    unnamed x20, local copies, waits for them, and re-layouts  39.3 us
    all_gather x1, waiting for transfers between devices, per_device(): lax.all_gather(w_down, 'grp', axis=1, tiled=True)  35.5 us
    unnamed x1, other arithmetic  32 us
  transfers between devices with their start and end apart: 6, of which 5 were waited for; matrix products, arithmetic and copies ran while one was open for 10% of the time, Pallas kernels for 0%

commit v1 on v0

--- a/solution.py
+++ b/solution.py
@@ -115,7 +115,10 @@
         lax.all_gather(w_down, "grp", axis=1, tiled=True),
         preferred_element_type=jnp.float32,
     ).astype(jnp.bfloat16)
-    returned = lax.all_to_all(expert_out, "dev", split_axis=1, concat_axis=0, tiled=True)
+    returned = jnp.concatenate(
+        lax.all_to_all(jnp.stack(jnp.split(expert_out, lax.axis_size("dev"), axis=1)), "dev", 0, 0),
+        axis=0,
+    )
     returned = returned.reshape(EXPERTS * slot_count, D)
     back_hits = place[:, :, None] == slot_ids[None, None, :]
     ctable = jnp.sum(

time: 976 us -> 882 us (0.904)
  local copies, waits for them, and re-layouts: 124 us -> 64.1 us
  other arithmetic: 63.1 us -> 31.1 us
    convert_element_type x1 -> x0, local copies, waits for them, and re-layouts: 52.2 us -> none  [per_device(): expert_out = jnp.einsum('erf,efd->erd', sliced, lax.all_gather(w_down, 'g...]
    unnamed x1 -> x0, other arithmetic: 32 us -> none
    unnamed x20 -> x48, local copies, waits for them, and re-layouts: 39.3 us -> 31.2 us
  transfers between devices with their start and end apart: 6 -> 6, of which waited for: 5 -> 5; matrix products, arithmetic and copies ran while one was open for 10% -> 11% of each run, Pallas kernels for 0% -> 0%
where the time goes in v1:
time: 882 us; the launch traced here: 881 us
  waiting for transfers between devices  700 us (79%)
  local copies, waits for them, and re-layouts  64.1 us (7%)
  matrix products  49.4 us (6%)
  other arithmetic  31.1 us (4%)
  starting transfers between devices  21 us (2%)
  between operations  15.1 us (2%)
    all_gather x1, waiting for transfers between devices, per_device(): lax.all_gather(o_weight, ('grp', 'dev'), axis=0, tiled=True)  355 us
    all_gather x1, waiting for transfers between devices, per_device(): lax.all_gather(w_gate_up, 'grp', axis=1, tiled=True)  160 us
    all_to_all x1, waiting for transfers between devices, per_device(): lax.all_to_all(jnp.stack(jnp.split(expert_out, lax.axis_size('dev'), axis...  105 us
    all_gather x1, waiting for transfers between devices, per_device(): piece = lax.all_gather(prefix_kv[0], 'dev', axis=0, tiled=True)  42.5 us
    all_gather x1, waiting for transfers between devices, per_device(): lax.all_gather(w_down, 'grp', axis=1, tiled=True)  35.5 us
    unnamed x48, local copies, waits for them, and re-layouts  31.2 us
    slice x3, local copies, waits for them, and re-layouts, per_device(): carry = update(initial, piece[:, 0], piece[:, 1], None)  29.5 us
  transfers between devices with their start and end apart: 6, of which 5 were waited for; matrix products, arithmetic and copies ran while one was open for 11% of the time, Pallas kernels for 0%

profile of v1, /device:TPU:1, one launch (start us, length us, event | category | flops | bytes accessed | tf_op | source)
XLA Modules:
  0.0 881.0 jit_solution(167029845837824428)
XLA Ops:
  7.4 0.7 all-gather.11.cloned.1.call-update
  8.1 0.7 all-gather.13.cloned.1.call-update
  8.8 0.8 copy.79
  9.8 1.2 copy.73
  11.0 1.5 fusion.78
  12.9 9.0 %reduce-window.6 = s32[32,8,128]{2,1,0:T(8,128)S(1)} reduce-window(s32[32,8,128]{2,1,0:T(8,128)S(1)} %fusion.65, s32[]{:T(128)} %constant.5.clone.1), window={size=1x1x128 pad=0_0x0_0x127_0}, to_apply=%region_4.5 | reduce-window | flops 4161536 | bytes 262148 | tf_op jit(solution)/shard_map/reduce-window
  22.6 0.7 multiply_add_fusion
  23.3 8.0 convert_reduce_fusion
  31.4 1.6 fusion.79
  33.0 42.5 %all-gather.11.cloned.1.call-done = bf16[1,2048,2,512]{3,2,0,1:T(2,128)(2,1)} async-done(((bf16[1,64,2,512]{3,2,0,1:T(2,128)(2,1)}), bf16[1,2048,2,512]{3,2,0,1:T(2,128)(2,1)}) %all-gather.11.cloned.1.call-update) | async-done | bytes 4194320 | tf_op jit(solution)/shard_map/all_gather | solution.py:66
  75.5 9.9 %fusion.77 = (bf16[2048,1,512]{2,1,0:T(2,128)(2,1)}, bf16[2048,1,512]{2,1,0:T(2,128)(2,1)}) fusion(bf16[2048,2,512]{2,1,0:T(2,128)(2,1)} %bitcast.255), kind=kLoop, calls=%fused_computation.133 | loop fusion | bytes 8388608 | tf_op jit(solution)/shard_map/slice | solution.py:67
  85.4 10.6 %copy.74 = bf16[2048,1,512]{0,2,1:T(8,128)(2,1)} copy(bf16[2048,1,512]{2,1,0:T(2,128)(2,1)} %get-tuple-element.8) | data formatting | bytes 4194304 | tf_op jit(solution)/shard_map/slice | solution.py:67
  96.0 9.0 %copy.72 = bf16[2048,1,512]{0,2,1:T(8,128)(2,1)S(1)} copy(bf16[2048,1,512]{2,1,0:T(2,128)(2,1)} %get-tuple-element.7) | data formatting | bytes 4194304 | tf_op jit(solution)/shard_map/slice | solution.py:67
  105.0 10.1 %bitcast_reduce_fusion = (f32[8,3,128]{2,1,0:T(4,128)S(1)}, f32[8,2048,128,3]{2,1,3,0:T(8,128)}) fusion(bf16[2048,8,64,1]{0,2,3,1:T(8,128)(2,1)S(1)} %bitcast.256, bf16[128,8,3,64]{0,3,2,1:T(8,128)(2,1)S(1)} %bitcast.259), kind=kOutput, calls=%fused_computation.1 | convolution fusion | flops 817886208 | bytes 27668480 | tf_op jit(solution)/shard_map/tgrd,ngd->grtn/dot_general | solution.py:39
  115.4 10.6 %fusion.1 = f32[8,3,128]{2,1,0:T(4,128)S(1)} fusion(f32[8,2048,128,3]{2,1,3,0:T(8,128)} %get-tuple-element.17, f32[8,3,128]{2,1,0:T(4,128)S(1)} %get-tuple-element.13), kind=kLoop, calls=%fused_computation.3 | loop fusion | flops 18871296 | bytes 25190400 | tf_op jit(solution)/shard_map/reduce_sum | solution.py:52
  126.1 10.5 %fusion.22 = f32[128,8,3,64]{0,3,2,1:T(8,128)S(1)} fusion(bf16[2048,8,64,1]{0,2,3,1:T(8,128)(2,1)S(1)} %bitcast.257, f32[8,2048,128,3]{2,1,3,0:T(8,128)} %get-tuple-element.17, f32[8,3,128]{2,1,0:T(4,128)S(1)} %get-tuple-element.13, f32[128,8,3]{0,2,1:T(4,128)S(1)} %get-tuple-element.6, f32[128,8,3]{0,2,1:T(4,128)S(1)} %get-tuple-element.11), kind=kOutput, calls=%fused_computation.31 | convolution fusion | flops 824573952 | bytes 28086272 | tf_op jit(solution)/shard_map/grtn,ngd->grtd/dot_general | solution.py:53
  137.0 354.9 %all-gather.13.cloned.1.call-done = bf16[256,6,1536]{2,1,0:T(8,128)(2,1)} async-done(((bf16[1,6,1536]{2,1,0:T(8,128)(2,1)}), bf16[256,6,1536]{2,1,0:T(8,128)(2,1)}) %all-gather.13.cloned.1.call-update) | async-done | bytes 4718608 | tf_op jit(solution)/shard_map/all_gather | solution.py:80
  491.9 8.4 reshape.168
  500.4 3.2 multiply_reduce_fusion
  503.6 3.6 convolution_convert_fusion.1
  507.2 9.9 %all-to-all-start = ((bf16[32,48,1536]{2,1,0:T(8,128)(2,1)}), bf16[32,48,1536]{2,1,0:T(8,128)(2,1)}, u32[]{:S(2)}, u32[]{:S(2)}) async-start(bf16[32,48,1536]{2,1,0:T(8,128)(2,1)} %bitcast.254), calls=%async_computation | async-start | bytes 9437184 | tf_op jit(solution)/shard_map/all_to_all | solution.py:102
  518.3 160.1 %all-gather.7.cloned.1.call-done = bf16[1,1536,1024]{2,1,0:T(8,128)(2,1)} async-done(((bf16[1,192,1024]{2,1,0:T(8,128)(2,1)}), bf16[1,1536,1024]{2,1,0:T(8,128)(2,1)}) %all-gather.7.cloned.1.call-update) | async-done | bytes 3145744 | tf_op jit(solution)/shard_map/all_gather | solution.py:107
  678.4 9.8 %convolution_bitcast_fusion = f32[1,1536,1024]{2,1,0:T(8,128)} fusion(bf16[1536,1536]{1,0:T(8,128)(2,1)} %bitcast.29, bf16[1,1536,1024]{2,1,0:T(8,128)(2,1)} %all-gather.7.cloned.1.call-done), kind=kOutput, calls=%fused_computation.13 | convolution fusion | flops 4831838208 | bytes 14155776 | tf_op jit(solution)/shard_map/erd,edf->erf/dot_general | solution.py:104
  688.2 35.5 %all-gather.9.cloned.1.call-done = bf16[1,512,1536]{2,1,0:T(8,128)(2,1)} async-done(((bf16[1,64,1536]{2,1,0:T(8,128)(2,1)}), bf16[1,512,1536]{2,1,0:T(8,128)(2,1)}) %all-gather.9.cloned.1.call-update) | async-done | bytes 1572880 | tf_op jit(solution)/shard_map/all_gather | solution.py:115
  723.7 6.0 fusion.5
  729.7 0.7 fusion.61
  735.7 0.7 fusion.52
  745.7 0.7 fusion.37
  751.2 11.0 %all-to-all-start.1 = ((bf16[32,1,48,1536]{3,2,1,0:T(8,128)(2,1)}), bf16[32,1,48,1536]{3,2,1,0:T(8,128)(2,1)}, u32[]{:S(2)}, u32[]{:S(2)}) async-start(bf16[32,1,48,1536]{3,2,1,0:T(8,128)(2,1)} %fusion.30), calls=%async_computation.1 | async-start | bytes 9437184 | tf_op jit(solution)/shard_map/all_to_all | solution.py:119
  762.8 2.1 select_reduce_fusion
  764.8 104.9 %all-to-all-done.1 = bf16[32,1,48,1536]{3,2,1,0:T(8,128)(2,1)} async-done(((bf16[32,1,48,1536]{3,2,1,0:T(8,128)(2,1)}), bf16[32,1,48,1536]{3,2,1,0:T(8,128)(2,1)}, u32[]{:S(2)}, u32[]{:S(2)}) %all-to-all-start.1) | async-done | bytes 4718624 | tf_op jit(solution)/shard_map/all_to_all | solution.py:119
  869.7 3.9 fusion.8
  (76 shorter events, 23.2 us)
Async XLA Ops:
  7.4 754.9 %copy-start = (bf16[1536,32]{0,1:T(8,128)(2,1)S(1)}, bf16[1536,32]{0,1:T(8,128)(2,1)}, u32[]{:S(2)}) copy-start(bf16[1536,32]{0,1:T(8,128)(2,1)} %param.18) | copy-start | bytes 294916
  7.4 24.0 %copy-start.6 = (s32[1,128]{1,0:T(1,128)S(1)}, s32[1,128]{1,0:T(1,128)}, u32[]{:S(2)}) copy-start(s32[1,128]{1,0:T(1,128)} %param.15) | copy-start | bytes 1540
  7.4 68.1 %all-gather.11.cloned.1.call-start = ((), (), s32[]{:S(2)}) async-start(), calls=%async_computation.4 | async-start | bytes 4325376 | tf_op jit(solution)/shard_map/all_gather | solution.py:66
  8.1 483.8 %all-gather.13.cloned.1.call-start = ((), (), s32[]{:S(2)}) async-start(), calls=%async_computation.5 | async-start | bytes 6316032 | tf_op jit(solution)/shard_map/all_gather | solution.py:80
  105.0 10.2 %copy-start.2 = (f32[8,3,128,128]{2,3,1,0:T(8,128)S(1)}, f32[8,3,128,128]{2,3,1,0:T(8,128)}, u32[]{:S(2)}) copy-start(f32[8,3,128,128]{2,3,1,0:T(8,128)} %get-tuple-element.15) | copy-start | bytes 4718596
  115.4 10.7 %copy-start.1 = (bf16[2048,1,512]{0,2,1:T(8,128)(2,1)S(1)}, bf16[2048,1,512]{0,2,1:T(8,128)(2,1)}, u32[]{:S(2)}) copy-start(bf16[2048,1,512]{0,2,1:T(8,128)(2,1)} %copy.74) | copy-start | bytes 6291460
  137.0 363.3 %copy-start.3 = (bf16[128,1536]{1,0:T(8,128)(2,1)S(1)}, bf16[128,1536]{1,0:T(8,128)(2,1)}, u32[]{:S(2)}) copy-start(bf16[128,1536]{1,0:T(8,128)(2,1)} %param.11) | copy-start | bytes 1179652
  500.3 3.3 copy-start.5
  507.2 171.2 %all-to-all-start = ((bf16[32,48,1536]{2,1,0:T(8,128)(2,1)}), bf16[32,48,1536]{2,1,0:T(8,128)(2,1)}, u32[]{:S(2)}, u32[]{:S(2)}) async-start(bf16[32,48,1536]{2,1,0:T(8,128)(2,1)} %bitcast.254), calls=%async_computation | async-start | bytes 9437184 | tf_op jit(solution)/shard_map/all_to_all | solution.py:102
  517.1 161.3 %all-gather.7.cloned.1.call-start = ((), (), s32[]{:S(2)}) async-start(), calls=%async_computation.2 | async-start | bytes 3538944 | tf_op jit(solution)/shard_map/all_gather | solution.py:107
  517.7 206.0 %all-gather.9.cloned.1.call-start = ((), (), s32[]{:S(2)}) async-start(), calls=%async_computation.3 | async-start | bytes 1769472 | tf_op jit(solution)/shard_map/all_gather | solution.py:115
  751.2 11.4 %copy-start.4 = (s32[128,8]{0,1:T(8,128)S(1)}, s32[128,8]{0,1:T(8,128)}, u32[]{:S(2)}) copy-start(s32[128,8]{0,1:T(8,128)} %param.19) | copy-start | bytes 12292
  751.2 118.6 %all-to-all-start.1 = ((bf16[32,1,48,1536]{3,2,1,0:T(8,128)(2,1)}), bf16[32,1,48,1536]{3,2,1,0:T(8,128)(2,1)}, u32[]{:S(2)}, u32[]{:S(2)}) async-start(bf16[32,1,48,1536]{3,2,1,0:T(8,128)(2,1)} %fusion.30), calls=%async_computation.1 | async-start | bytes 9437184 | tf_op jit(solution)/shard_map/all_to_all | solution.py:119
Sparse Core Ops, SparseCore 0:
  10.7 64.6 all-gather.10
  77.4 414.5 all-gather.12
Sparse Core Ops, SparseCore 1:
  519.4 159.0 all-gather.6
  680.1 43.6 all-gather.8
